TPU v7x, 32 devices: a whole 2x2x4 slice. The times are simulated.
32 devices in a mesh: mode: 2 (over x), space: 16 (over z, y, core).
Axes of the slice: x: 2, y: 2, z: 4, core: 2. Of those that a mesh axis runs over, the one named last changes fastest.
Arguments:
- field: bfloat16 [64, 256, 1024], P('mode', 'space'), may hold values from -6 to 6
- kappa_x: float32 [8, 256, 1024], P(None, 'space'), may hold values from -4 to 4
- kappa_y: float32 [8, 256, 1024], P(None, 'space'), may hold values from -4 to 4
- coupling: bfloat16 [4, 8, 32, 32], P('mode'), may hold values from -0.625 to 0.625
- pattern: int32 [4, 8, 32, 32], P('mode'), may hold values 0 or 1
Outputs:
- image: float32 [64, 256, 1024], P('mode', 'space')
All inputs are finite; a program needn't handle non-finite values. No bound on the sum of `pattern` on one device may be relied on, other than what follows from the above.
Results may differ from a plain program's by a relative error of at most 0.0003.
Values may be sent and summed in bfloat16 or wider, within the bound.
A program may use at most 64 MiB of HBM per device.

v0:
```python
import jax
import jax.numpy as jnp
from jax import lax
from jax.sharding import PartitionSpec as P


def from_behind(value, axis, steps):
    count = lax.axis_size(axis)
    initial, last = (max(0, -steps), min(count, count - steps))
    return lax.ppermute(value, axis, [(source, source + steps) for source in range(initial, last)])


def passed_along(x, axis, by):
    size = lax.axis_size(axis)
    return lax.ppermute(x, axis, [(i, (i + by) % size) for i in range(size)])


def stacked_mix(tiles, blocks):
    wide = jnp.concatenate(tiles, axis=1)
    tall = jnp.concatenate(blocks, axis=0)
    return jnp.einsum("ij,jrw->irw", wide, tall, preferred_element_type=jnp.float32)


def fluxes(term_of, kappa_x, kappa_y):
    kmodes = kappa_x.shape[0]
    flux_x = None
    flux_y = None
    for k in range(kmodes):
        wk = term_of(k)
        rows = wk.shape[1] - 1
        inner = wk[:, :rows, :]
        diff_x = wk[:, 1:, :] - inner
        next_col = jnp.concatenate(
            [inner[:, :, 1:], jnp.zeros((inner.shape[0], rows, 1), jnp.float32)], axis=2
        )
        part_x = kappa_x[k] * diff_x
        part_y = kappa_y[k] * (next_col - inner)
        flux_x = part_x if flux_x is None else flux_x + part_x
        flux_y = part_y if flux_y is None else flux_y + part_y
    return (flux_x, flux_y)


def divergence(flux_x, flux_y, below):
    prev_x = jnp.concatenate([below, flux_x[:, :-1, :]], axis=1)
    prev_y = jnp.concatenate(
        [jnp.zeros(flux_y.shape[:2] + (1,), jnp.float32), flux_y[:, :, :-1]], axis=2
    )
    return -(flux_x - prev_x) - (flux_y - prev_y)


def shards(field, kappa_x, kappa_y, coupling, pattern):
    coef = jnp.where(pattern > 0, coupling, jnp.zeros(coupling.shape, jnp.bfloat16))
    half = coef[0] * 0.5
    rim = from_behind(field[:, :1, :], "space", -1)
    extended = jnp.concatenate([field, rim], axis=1)
    uppers = []
    lowers = []
    lower_coefs = []
    uppers.append(passed_along(extended, "mode", -1))
    low_block, low_coef = passed_along((extended, coef[1]), "mode", 1)
    lowers.append(low_block)
    lower_coefs.append(low_coef)

    def term_of(k):
        tiles = [half[k], half[k].T]
        blocks = [extended, extended]
        tiles.append(coef[1, k])
        blocks.append(uppers[0])
        tiles.append(lower_coefs[0][k].T)
        blocks.append(lowers[0])
        return stacked_mix(tiles, blocks)

    flux_x, flux_y = fluxes(term_of, kappa_x, kappa_y)
    below = from_behind(flux_x[:, -1:, :], "space", 1)
    image = divergence(flux_x, flux_y, below)
    return image


def solution(mesh):
    placed = (
        P("mode", "space", None),
        P(None, "space", None),
        P(None, "space", None),
        P("mode", None, None, None),
        P("mode", None, None, None),
    )
    return jax.shard_map(
        shards, mesh=mesh, in_specs=placed, out_specs=P("mode", "space", None), check_vma=False
    )
```

profile of v0, /device:TPU:0, one launch (start us, length us, event | category | flops | bytes accessed | tf_op | source)
XLA Modules:
  0.0 97.8 jit_solution(10261340495498823770)
XLA Ops:
  0.0 1.2 %slice.309 = bf16[32,1,1024]{2,1,0:T(2,128)(2,1)S(1)} slice(bf16[32,16,1024]{2,1,0:T(8,128)(2,1)} %param.5), slice={[0:32], [0:1], [0:1024]} | slice | bytes 131072 | tf_op jit(solution)/shard_map/slice | solution.py:54
  1.3 1.3 %collective-permute-start.1 = (bf16[32,1,1024]{2,0,1:T(8,128)(2,1)S(1)}, bf16[32,1,1024]{2,0,1:T(8,128)(2,1)}, u32[]{:S(2)}, u32[]{:S(2)}) collective-permute-start(bf16[32,1,1024]{2,0,1:T(8,128)(2,1)S(1)} %copy.49), channel_id=1, source_target_pairs={{1,0},{2,1},{3,2},{4,3},{5,4},{6,5},{7,6},{8,7},{9,8},{10,9},{11,1... | collective-permute-start | bytes 196616 | tf_op jit(solution)/shard_map/ppermute | solution.py:10
  2.6 1.1 %compare_select_fusion = bf16[2,8,32,32]{3,2,1,0:T(8,128)(2,1)S(1)} fusion(bf16[2,8,32,32]{3,2,1,0:T(8,128)(2,1)} %param.8, s32[2,8,32,32]{3,2,1,0:T(8,128)} %param.9), kind=kLoop, calls=%fused_computation.28 | loop fusion | flops 32768 | bytes 131072 | tf_op jit(solution)/shard_map/jit(_where)/select_n | solution.py:52
  4.4 3.0 %collective-permute-start = (bf16[8,32,32]{1,2,0:T(8,128)(2,1)}, bf16[8,32,32]{1,2,0:T(8,128)(2,1)}, u32[]{:S(2)}, u32[]{:S(2)}) collective-permute-start(bf16[8,32,32]{1,2,0:T(8,128)(2,1)} %copy.35), channel_id=1, source_target_pairs={{0,16},{16,0},{1,17},{17,1},{2,18},{18,2},{3,19},{19,3},{4,20},{20... | collective-permute-start | bytes 49160 | tf_op jit(solution)/shard_map/ppermute | solution.py:15
  8.1 0.8 constant_dynamic-update-slice_fusion
  9.0 0.9 slice_bitcast_fusion.8
  9.9 0.8 slice_bitcast_fusion.16
  12.6 0.8 slice_bitcast_fusion.31
  13.4 22.9 %collective-permute-done.2 = bf16[32,17,1024]{2,0,1:T(8,128)(2,1)} collective-permute-done((bf16[32,17,1024]{2,0,1:T(8,128)(2,1)S(1)}, bf16[32,17,1024]{2,0,1:T(8,128)(2,1)}, u32[]{:S(2)}, u32[]{:S(2)}) %collective-permute-start.2) | collective-permute-done | bytes 1114144 | tf_op jit(solution)/shard_map/ppermute | solution.py:15
  36.3 2.3 %fusion.17 = f32[32,17,1024]{2,0,1:T(8,128)S(1)} fusion(bf16[32,32]{1,0:T(8,128)(2,1)S(1)} %get-tuple-element.47, bf16[32,32]{1,0:T(8,128)(2,1)S(1)} %get-tuple-element.21, bf16[32,32]{1,0:T(8,128)(2,1)S(1)} %get-tuple-element.32, bf16[32,32]{1,0:T(8,128)(2,1)S(1)} %copy.36, bf16[32,17,1024]{2,0,1:T(8,128)(2,1)} %collective-permute-done.2, ...), kind=kOutput, calls=%fused_computation.64 | convolution fusion | flops 160464896 | bytes 4464640 | tf_op jit(solution)/shard_map/ij,jrw->irw/dot_general | solution.py:21
  38.6 2.0 %slice.349 = f32[32,16,1023]{2,0,1:T(8,128)} slice(f32[32,17,1024]{2,0,1:T(8,128)S(1)} %fusion.17), slice={[0:32], [0:16], [1:1024]} | slice | bytes 4190208 | tf_op jit(solution)/shard_map/slice | solution.py:34
  40.6 2.3 %fusion.24 = f32[32,17,1024]{2,0,1:T(8,128)S(1)} fusion(bf16[32,32]{1,0:T(8,128)(2,1)S(1)} %get-tuple-element.54, bf16[32,32]{1,0:T(8,128)(2,1)S(1)} %get-tuple-element.28, bf16[32,32]{1,0:T(8,128)(2,1)S(1)} %get-tuple-element.33, bf16[32,32]{1,0:T(8,128)(2,1)S(1)} %copy.39, bf16[32,17,1024]{2,0,1:T(8,128)(2,1)} %collective-permute-done.2, ...), kind=kOutput, calls=%fused_computation.72 | convolution fusion | flops 160464896 | bytes 4464640 | tf_op jit(solution)/shard_map/ij,jrw->irw/dot_general | solution.py:21
  42.8 1.9 %slice.350 = f32[32,16,1023]{2,0,1:T(8,128)} slice(f32[32,17,1024]{2,0,1:T(8,128)S(1)} %fusion.24), slice={[0:32], [0:16], [1:1024]} | slice | bytes 4190208 | tf_op jit(solution)/shard_map/slice | solution.py:34
  44.8 2.3 %fusion.31 = f32[32,17,1024]{2,0,1:T(8,128)S(1)} fusion(bf16[32,32]{1,0:T(8,128)(2,1)S(1)} %get-tuple-element.53, bf16[32,32]{1,0:T(8,128)(2,1)S(1)} %get-tuple-element.27, bf16[32,32]{1,0:T(8,128)(2,1)S(1)} %get-tuple-element.34, bf16[32,32]{1,0:T(8,128)(2,1)S(1)} %copy.40, bf16[32,17,1024]{2,0,1:T(8,128)(2,1)} %collective-permute-done.2, ...), kind=kOutput, calls=%fused_computation.80 | convolution fusion | flops 160464896 | bytes 4464640 | tf_op jit(solution)/shard_map/ij,jrw->irw/dot_general | solution.py:21
  47.0 2.0 %slice.351 = f32[32,16,1023]{2,0,1:T(8,128)} slice(f32[32,17,1024]{2,0,1:T(8,128)S(1)} %fusion.31), slice={[0:32], [0:16], [1:1024]} | slice | bytes 4190208 | tf_op jit(solution)/shard_map/slice | solution.py:34
  49.0 2.3 %fusion.38 = f32[32,17,1024]{2,0,1:T(8,128)S(1)} fusion(bf16[32,32]{1,0:T(8,128)(2,1)S(1)} %get-tuple-element.52, bf16[32,32]{1,0:T(8,128)(2,1)S(1)} %get-tuple-element.26, bf16[32,32]{1,0:T(8,128)(2,1)S(1)} %get-tuple-element.35, bf16[32,32]{1,0:T(8,128)(2,1)S(1)} %copy.41, bf16[32,17,1024]{2,0,1:T(8,128)(2,1)} %collective-permute-done.2, ...), kind=kOutput, calls=%fused_computation.88 | convolution fusion | flops 160464896 | bytes 4464640 | tf_op jit(solution)/shard_map/ij,jrw->irw/dot_general | solution.py:21
  51.3 2.0 %slice.352 = f32[32,16,1023]{2,0,1:T(8,128)} slice(f32[32,17,1024]{2,0,1:T(8,128)S(1)} %fusion.38), slice={[0:32], [0:16], [1:1024]} | slice | bytes 4190208 | tf_op jit(solution)/shard_map/slice | solution.py:34
  53.3 2.3 %fusion.45 = f32[32,17,1024]{2,0,1:T(8,128)S(1)} fusion(bf16[32,32]{1,0:T(8,128)(2,1)S(1)} %get-tuple-element.51, bf16[32,32]{1,0:T(8,128)(2,1)S(1)} %get-tuple-element.25, bf16[32,32]{1,0:T(8,128)(2,1)S(1)} %get-tuple-element.36, bf16[32,32]{1,0:T(8,128)(2,1)S(1)} %copy.42, bf16[32,17,1024]{2,0,1:T(8,128)(2,1)} %collective-permute-done.2, ...), kind=kOutput, calls=%fused_computation.96 | convolution fusion | flops 160464896 | bytes 4464640 | tf_op jit(solution)/shard_map/ij,jrw->irw/dot_general | solution.py:21
  55.5 2.0 %slice.353 = f32[32,16,1023]{2,0,1:T(8,128)} slice(f32[32,17,1024]{2,0,1:T(8,128)S(1)} %fusion.45), slice={[0:32], [0:16], [1:1024]} | slice | bytes 4190208 | tf_op jit(solution)/shard_map/slice | solution.py:34
  57.5 2.3 %fusion.52 = f32[32,17,1024]{2,0,1:T(8,128)S(1)} fusion(bf16[32,32]{1,0:T(8,128)(2,1)S(1)} %get-tuple-element.50, bf16[32,32]{1,0:T(8,128)(2,1)S(1)} %get-tuple-element.24, bf16[32,32]{1,0:T(8,128)(2,1)S(1)} %get-tuple-element.37, bf16[32,32]{1,0:T(8,128)(2,1)S(1)} %copy.43, bf16[32,17,1024]{2,0,1:T(8,128)(2,1)} %collective-permute-done.2, ...), kind=kOutput, calls=%fused_computation.104 | convolution fusion | flops 160464896 | bytes 4464640 | tf_op jit(solution)/shard_map/ij,jrw->irw/dot_general | solution.py:21
  59.8 1.9 %slice.354 = f32[32,16,1023]{2,0,1:T(8,128)} slice(f32[32,17,1024]{2,0,1:T(8,128)S(1)} %fusion.52), slice={[0:32], [0:16], [1:1024]} | slice | bytes 4190208 | tf_op jit(solution)/shard_map/slice | solution.py:34
  61.7 2.3 %fusion.59 = f32[32,17,1024]{2,0,1:T(8,128)S(1)} fusion(bf16[32,32]{1,0:T(8,128)(2,1)S(1)} %get-tuple-element.49, bf16[32,32]{1,0:T(8,128)(2,1)S(1)} %get-tuple-element.23, bf16[32,32]{1,0:T(8,128)(2,1)S(1)} %get-tuple-element.38, bf16[32,32]{1,0:T(8,128)(2,1)S(1)} %copy.44, bf16[32,17,1024]{2,0,1:T(8,128)(2,1)} %collective-permute-done.2, ...), kind=kOutput, calls=%fused_computation.112 | convolution fusion | flops 160464896 | bytes 4464640 | tf_op jit(solution)/shard_map/ij,jrw->irw/dot_general | solution.py:21
  64.0 2.0 %slice.355 = f32[32,16,1023]{2,0,1:T(8,128)} slice(f32[32,17,1024]{2,0,1:T(8,128)S(1)} %fusion.59), slice={[0:32], [0:16], [1:1024]} | slice | bytes 4190208 | tf_op jit(solution)/shard_map/slice | solution.py:34
  66.0 2.2 %fusion.66 = f32[32,17,1024]{2,0,1:T(8,128)S(1)} fusion(bf16[32,32]{1,0:T(8,128)(2,1)S(1)} %get-tuple-element.48, bf16[32,32]{1,0:T(8,128)(2,1)S(1)} %copy-done.6, bf16[32,32]{1,0:T(8,128)(2,1)S(1)} %get-tuple-element.39, bf16[32,32]{1,0:T(8,128)(2,1)S(1)} %copy-done.7, bf16[32,17,1024]{2,0,1:T(8,128)(2,1)} %collective-permute-done.2, ...), kind=kOutput, calls=%fused_computation.120 | convolution fusion | flops 160464896 | bytes 4464640 | tf_op jit(solution)/shard_map/ij,jrw->irw/dot_general | solution.py:21
  68.2 1.9 %slice.356 = f32[32,16,1023]{2,0,1:T(8,128)} slice(f32[32,17,1024]{2,0,1:T(8,128)S(1)} %fusion.66), slice={[0:32], [0:16], [1:1024]} | slice | bytes 4190208 | tf_op jit(solution)/shard_map/slice | solution.py:34
  70.1 6.8 %fusion.1 = f32[32,16,1024]{2,0,1:T(8,128)} fusion(f32[32,17,1024]{2,0,1:T(8,128)S(1)} %fusion.66, f32[32,17,1024]{2,0,1:T(8,128)S(1)} %fusion.59, f32[32,17,1024]{2,0,1:T(8,128)S(1)} %fusion.52, f32[32,17,1024]{2,0,1:T(8,128)S(1)} %fusion.45, f32[32,17,1024]{2,0,1:T(8,128)S(1)} %fusion.38, f32[32,17,1024]{2,0,1:T(8,128)S(1)} %fusion.31, ...), kind=kLoop, calls=%fused_computation.3 | loop fusion | flops 12058624 | bytes 36175872 | tf_op jit(solution)/shard_map/add | solution.py:38
  76.9 1.6 %slice.347 = f32[32,1,1024]{2,0,1:T(8,128)} slice(f32[32,16,1024]{2,0,1:T(8,128)} %fusion.1), slice={[0:32], [15:16], [0:1024]} | slice | bytes 262144 | tf_op jit(solution)/shard_map/slice | solution.py:74
  78.5 2.5 %collective-permute-start.3 = (f32[32,1,1024]{2,0,1:T(8,128)}, f32[32,1,1024]{2,0,1:T(8,128)}, u32[]{:S(2)}, u32[]{:S(2)}) collective-permute-start(f32[32,1,1024]{2,0,1:T(8,128)} %slice.347), channel_id=1, source_target_pairs={{0,1},{1,2},{2,3},{3,4},{4,5},{5,6},{6,7},{7,8},{8,9},{9,10},{10,1... | collective-permute-start | bytes 393224 | tf_op jit(solution)/shard_map/ppermute | solution.py:10
  81.0 9.4 %multiply_add_fusion = f32[32,16,1024]{2,0,1:T(8,128)} fusion(f32[32,16,1023]{2,0,1:T(8,128)} %slice.356, f32[32,16,1023]{2,0,1:T(8,128)} %slice.355, f32[32,16,1023]{2,0,1:T(8,128)} %slice.354, f32[32,16,1023]{2,0,1:T(8,128)} %slice.353, f32[32,16,1023]{2,0,1:T(8,128)} %slice.352, f32[32,16,1023]{2,0,1:T(8,128)} %slice.351, f32[32,16,1023]{2,0,1:T(8,128)} %slice.350, ...), kind=kLoop, calls=%fused_computation.27 | loop fusion | flops 12058624 | bytes 36159488 | tf_op jit(solution)/shard_map/add | solution.py:39
  90.5 1.9 %slice.348 = f32[32,15,1024]{2,0,1:T(8,128)S(1)} slice(f32[32,16,1024]{2,0,1:T(8,128)} %fusion.1), slice={[0:32], [0:15], [0:1024]} | slice | bytes 3932160 | tf_op jit(solution)/shard_map/slice | solution.py:44
  92.6 2.6 %fusion.16 = f32[32,16,1024]{2,0,1:T(8,128)S(1)} fusion(f32[32,16,1024]{2,0,1:T(8,128)} %fusion.1, f32[32,15,1024]{2,0,1:T(8,128)S(1)} %slice.348, f32[32,1,1024]{2,0,1:T(8,128)} %collective-permute-done.3, f32[32,16,1024]{2,0,1:T(8,128)S(1)} %copy-done, f32[32,16,1023]{2,0,1:T(8,128)S(1)} %bitcast.147), kind=kLoop, calls=%fused_computation.26 | loop fusion | flops 2621440 | bytes 10483712 | tf_op jit(solution)/shard_map/sub | solution.py:48
  95.3 2.5 %copy.46 = f32[32,16,1024]{2,1,0:T(8,128)} copy(f32[32,16,1024]{2,0,1:T(8,128)S(1)} %fusion.16) | data formatting | bytes 4194304 | tf_op jit(solution)/shard_map/sub | solution.py:48
  (36 shorter events, 3.7 us)
Async XLA Ops:
  0.0 7.3 %copy-start.1 = (bf16[32,16,1024]{2,1,0:T(8,128)(2,1)S(1)}, bf16[32,16,1024]{2,1,0:T(8,128)(2,1)}, u32[]{:S(2)}) copy-start(bf16[32,16,1024]{2,1,0:T(8,128)(2,1)} %param.5) | copy-start | bytes 3145732
  0.0 9.0 %copy-start.4 = (f32[8,16,1024]{2,1,0:T(8,128)S(1)}, f32[8,16,1024]{2,1,0:T(8,128)}, u32[]{:S(2)}) copy-start(f32[8,16,1024]{2,1,0:T(8,128)} %param.7) | copy-start | bytes 1572868
  1.3 6.8 %collective-permute-start.1 = (bf16[32,1,1024]{2,0,1:T(8,128)(2,1)S(1)}, bf16[32,1,1024]{2,0,1:T(8,128)(2,1)}, u32[]{:S(2)}, u32[]{:S(2)}) collective-permute-start(bf16[32,1,1024]{2,0,1:T(8,128)(2,1)S(1)} %copy.49), channel_id=1, source_target_pairs={{1,0},{2,1},{3,2},{4,3},{5,4},{6,5},{7,6},{8,7},{9,8},{10,9},{11,1... | collective-permute-start | bytes 196616 | tf_op jit(solution)/shard_map/ppermute | solution.py:10
  3.6 6.2 %copy-start.5 = (f32[8,16,1024]{2,1,0:T(8,128)S(1)}, f32[8,16,1024]{2,1,0:T(8,128)}, u32[]{:S(2)}) copy-start(f32[8,16,1024]{2,1,0:T(8,128)} %param.6) | copy-start | bytes 1572868
  4.4 8.2 %collective-permute-start = (bf16[8,32,32]{1,2,0:T(8,128)(2,1)}, bf16[8,32,32]{1,2,0:T(8,128)(2,1)}, u32[]{:S(2)}, u32[]{:S(2)}) collective-permute-start(bf16[8,32,32]{1,2,0:T(8,128)(2,1)} %copy.35), channel_id=1, source_target_pairs={{0,16},{16,0},{1,17},{17,1},{2,18},{18,2},{3,19},{19,3},{4,20},{20... | collective-permute-start | bytes 49160 | tf_op jit(solution)/shard_map/ppermute | solution.py:15
  8.9 52.8 %copy-start.2 = (bf16[32,17,1024]{2,0,1:T(8,128)(2,1)}, bf16[32,17,1024]{2,0,1:T(8,128)(2,1)S(1)}, u32[]{:S(2)}) copy-start(bf16[32,17,1024]{2,0,1:T(8,128)(2,1)S(1)} %constant_dynamic-update-slice_fusion) | copy-start | bytes 3342340
  8.9 27.4 %collective-permute-start.2 = (bf16[32,17,1024]{2,0,1:T(8,128)(2,1)S(1)}, bf16[32,17,1024]{2,0,1:T(8,128)(2,1)}, u32[]{:S(2)}, u32[]{:S(2)}) collective-permute-start(bf16[32,17,1024]{2,0,1:T(8,128)(2,1)S(1)} %constant_dynamic-update-slice_fusion), channel_id=1, source_target_pairs={{0,16},{16,0},{1,17},{17,1},{2,18},{18,2},{3,19},{19,3},{4,20},{20... | collective-permute-start | bytes 3342344 | tf_op jit(solution)/shard_map/ppermute | solution.py:15
  64.0 2.0 %copy-start.3 = (bf16[32,17,1024]{2,0,1:T(8,128)(2,1)S(1)}, bf16[32,17,1024]{2,0,1:T(8,128)(2,1)}, u32[]{:S(2)}) copy-start(bf16[32,17,1024]{2,0,1:T(8,128)(2,1)} %copy-done.2) | copy-start | bytes 3342340
  64.0 2.0 %copy-start.6 = (bf16[32,32]{1,0:T(8,128)(2,1)S(1)}, bf16[32,32]{1,0:T(8,128)(2,1)}, u32[]{:S(2)}) copy-start(bf16[32,32]{1,0:T(8,128)(2,1)} %get-tuple-element.22) | copy-start | bytes 6148
  64.0 2.0 %copy-start.7 = (bf16[32,32]{1,0:T(8,128)(2,1)S(1)}, bf16[32,32]{1,0:T(8,128)(2,1)}, u32[]{:S(2)}) copy-start(bf16[32,32]{1,0:T(8,128)(2,1)} %copy.45) | copy-start | bytes 6148
  78.5 13.9 %collective-permute-start.3 = (f32[32,1,1024]{2,0,1:T(8,128)}, f32[32,1,1024]{2,0,1:T(8,128)}, u32[]{:S(2)}, u32[]{:S(2)}) collective-permute-start(f32[32,1,1024]{2,0,1:T(8,128)} %slice.347), channel_id=1, source_target_pairs={{0,1},{1,2},{2,3},{3,4},{4,5},{5,6},{6,7},{7,8},{8,9},{9,10},{10,1... | collective-permute-start | bytes 393224 | tf_op jit(solution)/shard_map/ppermute | solution.py:10
  90.5 2.2 %copy-start = (f32[32,16,1024]{2,0,1:T(8,128)S(1)}, f32[32,16,1024]{2,0,1:T(8,128)}, u32[]{:S(2)}) copy-start(f32[32,16,1024]{2,0,1:T(8,128)} %multiply_add_fusion) | copy-start | bytes 6291460
where the time goes:
time: 99.4 us; the launch traced here: 97.8 us
  local copies, waits for them, and re-layouts  29.9 us (30%)
  waiting for transfers between devices  22.9 us (23%)
  other arithmetic  19.9 us (20%)
  matrix products  18.1 us (18%)
  starting transfers between devices  6.81 us (7%)
    ppermute x2, waiting for transfers between devices, passed_along(): return lax.ppermute(x, axis, [(i, (i + by) % size) for i in range(size)])  22.9 us
    dot_general x8, matrix products, stacked_mix(): jnp.einsum('ij,jrw->irw', wide, tall, preferred_element_type=jnp.float32)  18.1 us
    slice x8, local copies, waits for them, and re-layouts, fluxes(): inner[:, :, 1:]  15.6 us
    add x1, other arithmetic, fluxes(): flux_y = part_y if flux_y is None else flux_y + part_y  9.41 us
    add x1, other arithmetic, fluxes(): flux_x = part_x if flux_x is None else flux_x + part_x  6.8 us
    ppermute x2, starting transfers between devices, from_behind(): lax.ppermute(value, axis, [(source, source + steps) for source in range(i...  3.84 us
    ppermute x2, starting transfers between devices, passed_along(): return lax.ppermute(x, axis, [(i, (i + by) % size) for i in range(size)])  2.97 us
    sub x1, other arithmetic, divergence(): return -(flux_x - prev_x) - (flux_y - prev_y)  2.62 us
  transfers between devices with their start and end apart: 4, of which 1 were waited for; matrix products, arithmetic and copies ran while one was open for 20% of the time, Pallas kernels for 0%

commit v1 on v0

v1 whole, which is shorter than its diff:
```python
import functools

import jax
import jax.numpy as jnp
from jax import lax
from jax.experimental import pallas as pl
from jax.experimental.pallas import tpu as pltpu
from jax.sharding import PartitionSpec as P

LANES = 256


def kernel(n_mode, n_space, u_hbm, kx_ref, ky_ref, a_ref, ct_hbm, kx_hbm, out_ref,
           u_ext, v_ext, ct_in, kx_in, fx_prev, fy_row, sh,
           local_sem, main_send, main_recv, halo_send, halo_recv):
    rows, mb, ny = u_hbm.shape
    terms = kx_ref.shape[0]
    sides = v_ext.shape[0]
    mode = lax.axis_index("mode")
    space = lax.axis_index("space")
    above = {"space": lax.rem(space + 1, n_space)}
    below = {"space": lax.rem(space + n_space - 1, n_space)}
    upper = {"mode": lax.rem(mode + 1, n_mode)}
    lower = {"mode": lax.rem(mode + n_mode - 1, n_mode)}

    barrier = pltpu.get_barrier_semaphore()
    for target in (above, below, upper, lower):
        pl.semaphore_signal(barrier, inc=1, device_id=target, device_id_type=pl.DeviceIdType.MESH)
    own = pltpu.make_async_copy(u_hbm, u_ext.at[pl.ds(1, rows)], local_sem)
    own.start()
    pl.semaphore_wait(barrier, 4)

    def remote(src, dst, send, recv, target):
        return pltpu.make_async_remote_copy(
            src_ref=src, dst_ref=dst, send_sem=send, recv_sem=recv,
            device_id=target, device_id_type=pl.DeviceIdType.MESH)

    towards = (lower, upper)

    def row_copy(side, r):
        return remote(u_hbm.at[r], v_ext.at[side, r + 1], main_send.at[side, r], main_recv.at[side, r], towards[side])

    def halo_up(side):
        return remote(v_ext.at[side, rows], v_ext.at[side, 0], halo_send.at[4 + side], halo_recv.at[4 + side], above)

    def halo_down(side):
        return remote(v_ext.at[side, 1], v_ext.at[side, rows + 1], halo_send.at[6 + side], halo_recv.at[6 + side], below)

    coef_copy = remote(ct_hbm, ct_in, halo_send.at[0], halo_recv.at[0], upper)
    last_copy = remote(u_hbm.at[rows - 1], u_ext.at[0], halo_send.at[1], halo_recv.at[1], above)
    first_copy = remote(u_hbm.at[0], u_ext.at[rows + 1], halo_send.at[2], halo_recv.at[2], below)
    kx_copy = remote(kx_hbm.at[:, pl.ds(rows - 8, 8), :], kx_in, halo_send.at[3], halo_recv.at[3], above)

    for side in range(sides):
        row_copy(side, rows - 1).start()
        row_copy(side, 0).start()
    coef_copy.start()
    last_copy.start()
    first_copy.start()
    kx_copy.start()
    for side in range(sides):
        @pl.loop(1, rows - 1)
        def _(r):
            row_copy(side, r).start()

    for side in range(sides):
        row_copy(side, rows - 1).wait_recv()
        halo_up(side).start()
        row_copy(side, 0).wait_recv()
        halo_down(side).start()
    own.wait()
    coef_copy.wait_recv()
    last_copy.wait_recv()
    first_copy.wait_recv()
    kx_copy.wait_recv()
    for side in range(sides):
        halo_up(side).wait_recv()
        halo_down(side).wait_recv()

    @pl.when(space == n_space - 1)
    def _():
        u_ext[rows + 1] = jnp.zeros((mb, ny), jnp.bfloat16)
        for side in range(sides):
            v_ext[side, rows + 1] = jnp.zeros((mb, ny), jnp.bfloat16)

    coef = a_ref[...] + ct_in[...]
    pair = jnp.concatenate([coef, -coef], axis=1)

    def stack(e, cols):
        u = u_ext[e, :, cols]
        vs = [v_ext[side, e, :, cols] for side in range(sides)]
        return [u, u, vs[0], vs[-1]]

    def weighted(diff, weight_of):
        total = None
        for k in range(terms):
            part = weight_of(k) * diff[k * mb:(k + 1) * mb]
            total = part if total is None else total + part
        return total

    def flux_x(e, cols, weight_of):
        diff = jnp.dot(pair, jnp.concatenate(stack(e + 1, cols) + stack(e, cols), axis=0),
                       preferred_element_type=jnp.float32)
        return weighted(diff, weight_of)

    blocks = [pl.ds(c, LANES) for c in range(0, ny, LANES)]
    keep = jnp.where(space == 0, 0.0, 1.0).astype(jnp.float32)
    for cols in blocks:
        fx_prev[:, cols] = flux_x(0, cols, lambda k: kx_in[k, 7:8, cols]) * keep

    def shifted(x):
        lane = lax.broadcasted_iota(jnp.int32, x.shape, 1)
        moved = pltpu.roll(x.astype(jnp.float32), ny - 1, axis=1)
        return jnp.where(lane == ny - 1, 0.0, moved).astype(jnp.bfloat16)

    def row(r):
        e = r + 1
        sh[0] = shifted(u_ext[e])
        for side in range(sides):
            sh[1 + side] = shifted(v_ext[side, e])
        for cols in blocks:
            fx = flux_x(e, cols, lambda k: kx_ref[k, pl.ds(r, 1), cols])
            ahead = [sh[0, :, cols]] * 2 + [sh[1, :, cols], sh[sides, :, cols]]
            diff = jnp.dot(pair, jnp.concatenate(ahead + stack(e, cols), axis=0),
                           preferred_element_type=jnp.float32)
            fy = weighted(diff, lambda k: ky_ref[k, pl.ds(r, 1), cols])
            out_ref[r, :, cols] = fx_prev[:, cols] - fx - fy
            fx_prev[:, cols] = fx
            fy_row[:, cols] = fy
        fy = fy_row[...]
        lane = lax.broadcasted_iota(jnp.int32, fy.shape, 1)
        out_ref[r] += jnp.where(lane == 0, 0.0, pltpu.roll(fy, 1, axis=1))

    @pl.loop(0, rows - 3)
    def _(r):
        for side in range(sides):
            row_copy(side, r + 1).wait_recv()
        row(r)

    for side in range(sides):
        row_copy(side, rows - 2).wait_recv()

    @pl.loop(rows - 3, rows)
    def _(r):
        row(r)

    for side in range(sides):
        @pl.loop(0, rows)
        def _(r):
            row_copy(side, r).wait_send()
        halo_up(side).wait_send()
        halo_down(side).wait_send()
    for copy in (coef_copy, last_copy, first_copy, kx_copy):
        copy.wait_send()


def shards(n_mode, n_space, field, kappa_x, kappa_y, coupling, pattern):
    mb, rows, ny = field.shape
    terms = kappa_x.shape[0]
    sides = 1 if n_mode == 2 else 2
    coef = jnp.where(pattern > 0, coupling, jnp.zeros(coupling.shape, jnp.bfloat16))
    half = coef[0] * 0.5
    tall = lambda x: x.reshape(terms * mb, mb)
    flip = lambda x: tall(jnp.swapaxes(x, 1, 2))
    own = jnp.concatenate(
        [tall(half), flip(half), tall(coef[1]), jnp.zeros((terms * mb, mb), jnp.bfloat16)], axis=1)
    sent = jnp.concatenate(
        [jnp.zeros((terms * mb, 3 * mb), jnp.bfloat16), flip(coef[1])], axis=1)
    vmem = pl.BlockSpec(memory_space=pltpu.VMEM)
    hbm = pl.BlockSpec(memory_space=pl.ANY)
    out = pl.pallas_call(
        functools.partial(kernel, n_mode, n_space),
        out_shape=jax.ShapeDtypeStruct((rows, mb, ny), jnp.float32),
        in_specs=[hbm, vmem, vmem, vmem, hbm, hbm],
        out_specs=vmem,
        scratch_shapes=[
            pltpu.VMEM((rows + 2, mb, ny), jnp.bfloat16),
            pltpu.VMEM((sides, rows + 2, mb, ny), jnp.bfloat16),
            pltpu.VMEM((terms * mb, 4 * mb), jnp.bfloat16),
            pltpu.VMEM((terms, 8, ny), jnp.float32),
            pltpu.VMEM((mb, ny), jnp.float32),
            pltpu.VMEM((mb, ny), jnp.float32),
            pltpu.VMEM((1 + sides, mb, ny), jnp.bfloat16),
            pltpu.SemaphoreType.DMA,
            pltpu.SemaphoreType.DMA((sides, rows)),
            pltpu.SemaphoreType.DMA((sides, rows)),
            pltpu.SemaphoreType.DMA((8,)),
            pltpu.SemaphoreType.DMA((8,)),
        ],
        compiler_params=pltpu.CompilerParams(collective_id=0, has_side_effects=True),
    )(jnp.swapaxes(field, 0, 1), kappa_x, kappa_y, own, sent, kappa_x)
    return jnp.swapaxes(out, 0, 1)


def solution(mesh):
    placed = (
        P("mode", "space", None),
        P(None, "space", None),
        P(None, "space", None),
        P("mode", None, None, None),
        P("mode", None, None, None),
    )
    return jax.shard_map(
        functools.partial(shards, mesh.shape["mode"], mesh.shape["space"]),
        mesh=mesh, in_specs=placed, out_specs=P("mode", "space", None), check_vma=False)
```

time: 99.4 us -> 43.1 us (0.43); the launches traced: 97.8 us -> 42.9 us
  Pallas kernels: 0 us -> 34.3 us
  local copies, waits for them, and re-layouts: 29.9 us -> 6.68 us
  waiting for transfers between devices: 22.9 us -> 0 us
  matrix products: 18.1 us -> 0 us
  other arithmetic: 19.9 us -> 1.88 us
  starting transfers between devices: 6.81 us -> 0 us
    pallas_call x0 -> x1, Pallas kernels: none -> 34.3 us  [shards(): pl.pallas_call(functools.partial(kernel, n_mode, n_space), out_shape=jax....]
    ppermute x4 -> x0, waiting for transfers between devices: 22.9 us -> none  [the longest x2 22.9 us: passed_along(): return lax.ppermute(x, axis, [(i, (i + by) % size) for i in range(size)])]
    slice x12 -> x0, local copies, waits for them, and re-layouts: 20.3 us -> none  [the longest x8 15.6 us: fluxes(): inner[:, :, 1:]]
    dot_general x8 -> x0, matrix products: 18.1 us -> none  [stacked_mix(): jnp.einsum('ij,jrw->irw', wide, tall, preferred_element_type=jnp.float32)]
    add x2 -> x0, other arithmetic: 16.2 us -> none  [the longest x1 9.41 us: fluxes(): flux_y = part_y if flux_y is None else flux_y + part_y]
    ppermute x4 -> x0, starting transfers between devices: 6.81 us -> none  [the longest x2 3.84 us: from_behind(): lax.ppermute(value, axis, [(source, source + steps) for source in range(i...]
    transpose x1 -> x3, local copies, waits for them, and re-layouts: 0.82 us -> 4.33 us  [the longest x1 4.13 us: shards(): return jnp.swapaxes(out, 0, 1)]
    squeeze x11 -> x0, local copies, waits for them, and re-layouts: 2.65 us -> none  [the longest x9 1.33 us: term_of(): tiles = [half[k], half[k].T]]
  transfers between devices with their start and end apart: 4 -> 0, of which waited for: 1 -> 0; matrix products, arithmetic and copies ran while one was open for 20% -> 0% of each run, Pallas kernels for 0% -> 0%
where the time goes in v1:
time: 43.1 us; the launch traced here: 42.9 us
  Pallas kernels  34.3 us (80%)
  local copies, waits for them, and re-layouts  6.68 us (15%)
  other arithmetic  1.88 us (4%)
    pallas_call x1, Pallas kernels, shards(): pl.pallas_call(functools.partial(kernel, n_mode, n_space), out_shape=jax....  34.3 us
    transpose x1, local copies, waits for them, and re-layouts, shards(): return jnp.swapaxes(out, 0, 1)  4.13 us
    unnamed x3, local copies, waits for them, and re-layouts  1.55 us
    select_n x1, other arithmetic, shards(): jnp.where(pattern > 0, coupling, jnp.zeros(coupling.shape, jnp.bfloat16))  1.12 us

profile of v1, /device:TPU:0, one launch (start us, length us, event | category | flops | bytes accessed | tf_op | source)
XLA Modules:
  0.0 42.9 jit_solution(1883294561736876890)
XLA Ops:
  0.0 0.0 copy-start
  0.0 0.1 pad.4.clone
  0.1 1.1 %compare_select_fusion = bf16[2,8,32,32]{3,2,1,0:T(8,128)(2,1)S(1)} fusion(bf16[2,8,32,32]{3,2,1,0:T(8,128)(2,1)} %param.8, s32[2,8,32,32]{3,2,1,0:T(8,128)} %param.9), kind=kLoop, calls=%fused_computation.1 | loop fusion | flops 32768 | bytes 131072 | tf_op jit(solution)/shard_map/jit(_where)/select_n | solution.py:161
  1.2 0.1 copy.8
  1.3 0.7 %concatenate.7.ct_hbm = bf16[256,128]{1,0:T(8,128)(2,1)} pad(bf16[256,32]{1,0:T(8,128)(2,1)S(1)} %bitcast.18, bf16[]{:T(256)} %constant.4.clone.1), padding=0_0x96_0 | pad | bytes 81922 | tf_op jit(solution)/shard_map/concatenate | solution.py:167
  2.1 0.1 copy.7
  2.2 0.7 %maximum_maximum_fusion.a_ref = bf16[256,128]{1,0:T(8,128)(2,1)} fusion(bf16[256,32]{1,0:T(8,128)(2,1)S(1)} %bitcast.20, bf16[256,32]{1,0:T(8,128)(2,1)S(1)} %bitcast.19, bf16[256,32]{1,0:T(8,128)(2,1)S(1)} %bitcast.21, bf16[128]{0:T(256)(128)(2,1)S(1)} %pad.4.clone), kind=kLoop, calls=%fused_computation.3 | loop fusion | flops 262144 | bytes 114944 | tf_op jit(solution)/shard_map/concatenate | solution.py:165
  2.9 0.0 copy-done
  2.9 1.5 %copy.11 = bf16[32,16,1024]{2,0,1:T(8,128)(2,1)} copy(bf16[32,16,1024]{2,1,0:T(8,128)(2,1)S(1)} %copy-done) | data formatting | bytes 2097152 | tf_op args[0]
  4.4 34.3 %shard_map.55 = f32[16,32,1024]{2,1,0:T(8,128)} custom-call(bf16[16,32,1024]{2,1,0:T(8,128)(2,1)} %bitcast.17, f32[8,16,1024]{2,1,0:T(8,128)} %kx_hbm.1, f32[8,16,1024]{2,1,0:T(8,128)} %ky_ref.1, bf16[256,128]{1,0:T(8,128)(2,1)} %maximum_maximum_fusion.a_ref, bf16[256,128]{1,0:T(8,128)(2,1)} %concatenate.7.ct_hbm, f32[8,16,1024]{2,1,0:T(8,128)} %kx_hbm.1), custom_call_target="tpu_custom_call" | custom-call | tf_op jit(solution)/shard_map/pallas_call | solution.py:171
  38.8 4.1 %copy.9 = f32[32,16,1024]{2,1,0:T(8,128)} copy(f32[32,16,1024]{2,0,1:T(8,128)} %bitcast.16) | data formatting | bytes 4194304 | tf_op jit(solution)/shard_map/transpose | solution.py:192
  (2 shorter events, 0.0 us)
Async XLA Ops:
  0.0 2.9 %copy-start = (bf16[32,16,1024]{2,1,0:T(8,128)(2,1)S(1)}, bf16[32,16,1024]{2,1,0:T(8,128)(2,1)}, u32[]{:S(2)}) copy-start(bf16[32,16,1024]{2,1,0:T(8,128)(2,1)} %param.5) | copy-start | bytes 3145732

commit v2 on v1

--- a/solution.py
+++ b/solution.py
@@ -10,11 +10,12 @@
 LANES = 256
 
 
-def kernel(n_mode, n_space, u_hbm, kx_ref, ky_ref, a_ref, ct_hbm, kx_hbm, out_ref,
-           u_ext, v_ext, ct_in, kx_in, fx_prev, fy_row, sh,
+def kernel(n_mode, n_space, u_hbm, kx_hbm, ky_hbm, coup_hbm, pat_hbm, out_ref,
+           u_ext, v_ext, kx_ref, ky_ref, coup, pat, coup_in, pat_in, pair_ref,
+           kx_in, fx_prev, fy_row, held, last_row, sh,
            local_sem, main_send, main_recv, halo_send, halo_recv):
     rows, mb, ny = u_hbm.shape
-    terms = kx_ref.shape[0]
+    terms = kx_hbm.shape[0]
     sides = v_ext.shape[0]
     mode = lax.axis_index("mode")
     space = lax.axis_index("space")
@@ -26,8 +27,6 @@
     barrier = pltpu.get_barrier_semaphore()
     for target in (above, below, upper, lower):
         pl.semaphore_signal(barrier, inc=1, device_id=target, device_id_type=pl.DeviceIdType.MESH)
-    own = pltpu.make_async_copy(u_hbm, u_ext.at[pl.ds(1, rows)], local_sem)
-    own.start()
     pl.semaphore_wait(barrier, 4)
 
     def remote(src, dst, send, recv, target):
@@ -46,7 +45,8 @@
     def halo_down(side):
         return remote(v_ext.at[side, 1], v_ext.at[side, rows + 1], halo_send.at[6 + side], halo_recv.at[6 + side], below)
 
-    coef_copy = remote(ct_hbm, ct_in, halo_send.at[0], halo_recv.at[0], upper)
+    coup_copy = remote(coup_hbm.at[1], coup_in, halo_send.at[0], halo_recv.at[0], upper)
+    pat_copy = remote(pat_hbm.at[1], pat_in, halo_send.at[8], halo_recv.at[8], upper)
     last_copy = remote(u_hbm.at[rows - 1], u_ext.at[0], halo_send.at[1], halo_recv.at[1], above)
     first_copy = remote(u_hbm.at[0], u_ext.at[rows + 1], halo_send.at[2], halo_recv.at[2], below)
     kx_copy = remote(kx_hbm.at[:, pl.ds(rows - 8, 8), :], kx_in, halo_send.at[3], halo_recv.at[3], above)
@@ -54,7 +54,8 @@
     for side in range(sides):
         row_copy(side, rows - 1).start()
         row_copy(side, 0).start()
-    coef_copy.start()
+    coup_copy.start()
+    pat_copy.start()
     last_copy.start()
     first_copy.start()
     kx_copy.start()
@@ -62,14 +63,45 @@
         @pl.loop(1, rows - 1)
         def _(r):
             row_copy(side, r).start()
+
+    locals_ = [
+        pltpu.make_async_copy(src, dst, local_sem.at[i])
+        for i, (src, dst) in enumerate([
+            (coup_hbm, coup), (pat_hbm, pat), (u_hbm, u_ext.at[pl.ds(1, rows)]),
+            (kx_hbm, kx_ref), (ky_hbm, ky_ref)])]
+    for copy in locals_:
+        copy.start()
 
     for side in range(sides):
         row_copy(side, rows - 1).wait_recv()
         halo_up(side).start()
         row_copy(side, 0).wait_recv()
         halo_down(side).start()
-    own.wait()
-    coef_copy.wait_recv()
+    coup_copy.wait_recv()
+    pat_copy.wait_recv()
+    for copy in locals_:
+        copy.wait()
+
+    def masked(values, mask):
+        return jnp.where(mask > 0, values.astype(jnp.float32), 0.0)
+
+    def placed(block, slot, flip):
+        shape = (mb, 4 * mb)
+        spot = lax.broadcasted_iota(jnp.int32, shape, 0) + slot * mb
+        place = jnp.where(lax.broadcasted_iota(jnp.int32, shape, 1) == spot, 1.0, 0.0).astype(jnp.bfloat16)
+        return lax.dot_general(block.astype(jnp.bfloat16), place, (((0 if flip else 1,), (0,)), ((), ())),
+                               preferred_element_type=jnp.float32)
+
+    @pl.loop(0, terms)
+    def _(k):
+        half = masked(coup[0, k], pat[0, k]) * 0.5
+        coef = (placed(half, 0, False) + placed(half, 1, True)
+                + placed(masked(coup[1, k], pat[1, k]), 2, False)
+                + placed(masked(coup_in[k], pat_in[k]), 3, True)).astype(jnp.bfloat16)
+        at = pl.ds(pl.multiple_of(k * mb, mb), mb)
+        pair_ref[at, :4 * mb] = coef
+        pair_ref[at, 4 * mb:] = -coef
+
     last_copy.wait_recv()
     first_copy.wait_recv()
     kx_copy.wait_recv()
@@ -83,8 +115,7 @@
         for side in range(sides):
             v_ext[side, rows + 1] = jnp.zeros((mb, ny), jnp.bfloat16)
 
-    coef = a_ref[...] + ct_in[...]
-    pair = jnp.concatenate([coef, -coef], axis=1)
+    pair = pair_ref[...]
 
     def stack(e, cols):
         u = u_ext[e, :, cols]
@@ -113,36 +144,55 @@
         moved = pltpu.roll(x.astype(jnp.float32), ny - 1, axis=1)
         return jnp.where(lane == ny - 1, 0.0, moved).astype(jnp.bfloat16)
 
-    def row(r):
+    def kx_row(r, cols):
+        return lambda k: kx_ref[k, pl.ds(r, 1), cols]
+
+    def flux_y_part(r):
         e = r + 1
         sh[0] = shifted(u_ext[e])
         for side in range(sides):
             sh[1 + side] = shifted(v_ext[side, e])
         for cols in blocks:
-            fx = flux_x(e, cols, lambda k: kx_ref[k, pl.ds(r, 1), cols])
             ahead = [sh[0, :, cols]] * 2 + [sh[1, :, cols], sh[sides, :, cols]]
             diff = jnp.dot(pair, jnp.concatenate(ahead + stack(e, cols), axis=0),
                            preferred_element_type=jnp.float32)
-            fy = weighted(diff, lambda k: ky_ref[k, pl.ds(r, 1), cols])
-            out_ref[r, :, cols] = fx_prev[:, cols] - fx - fy
-            fx_prev[:, cols] = fx
-            fy_row[:, cols] = fy
+            fy_row[:, cols] = weighted(diff, lambda k: ky_ref[k, pl.ds(r, 1), cols])
         fy = fy_row[...]
         lane = lax.broadcasted_iota(jnp.int32, fy.shape, 1)
-        out_ref[r] += jnp.where(lane == 0, 0.0, pltpu.roll(fy, 1, axis=1))
+        return jnp.where(lane == 0, 0.0, pltpu.roll(fy, 1, axis=1)) - fy
+
+    def put(r, cols, value):
+        for at in range(0, LANES, 128):
+            tile = (cols.start + at) // 128
+            start = (r // 8) * 8 * (ny // 128) + tile * 8 + r % 8
+            out_ref[pl.ds(start, mb, stride=rows * (ny // 128)), :] = value[:, at:at + 128]
+
+    def flux_x_step(r):
+        for cols in blocks:
+            fx = flux_x(r + 1, cols, kx_row(r, cols))
+            put(r, cols, fx_prev[:, cols] - fx + held[:, cols])
+            fx_prev[:, cols] = fx
+
+    final = rows - 1
+    last_row[...] = flux_y_part(final)
+    for cols in blocks:
+        last_row[:, cols] = last_row[:, cols] - flux_x(rows, cols, kx_row(final, cols))
 
     @pl.loop(0, rows - 3)
     def _(r):
+        held[...] = flux_y_part(r)
         for side in range(sides):
             row_copy(side, r + 1).wait_recv()
-        row(r)
-
+        flux_x_step(r)
+
+    held[...] = flux_y_part(rows - 3)
     for side in range(sides):
         row_copy(side, rows - 2).wait_recv()
-
-    @pl.loop(rows - 3, rows)
-    def _(r):
-        row(r)
+    flux_x_step(rows - 3)
+    held[...] = flux_y_part(rows - 2)
+    flux_x_step(rows - 2)
+    for cols in blocks:
+        put(final, cols, last_row[:, cols] + fx_prev[:, cols])
 
     for side in range(sides):
         @pl.loop(0, rows)
@@ -150,7 +200,7 @@
             row_copy(side, r).wait_send()
         halo_up(side).wait_send()
         halo_down(side).wait_send()
-    for copy in (coef_copy, last_copy, first_copy, kx_copy):
+    for copy in (coup_copy, pat_copy, last_copy, first_copy, kx_copy):
         copy.wait_send()
 
 
@@ -158,38 +208,39 @@
     mb, rows, ny = field.shape
     terms = kappa_x.shape[0]
     sides = 1 if n_mode == 2 else 2
-    coef = jnp.where(pattern > 0, coupling, jnp.zeros(coupling.shape, jnp.bfloat16))
-    half = coef[0] * 0.5
-    tall = lambda x: x.reshape(terms * mb, mb)
-    flip = lambda x: tall(jnp.swapaxes(x, 1, 2))
-    own = jnp.concatenate(
-        [tall(half), flip(half), tall(coef[1]), jnp.zeros((terms * mb, mb), jnp.bfloat16)], axis=1)
-    sent = jnp.concatenate(
-        [jnp.zeros((terms * mb, 3 * mb), jnp.bfloat16), flip(coef[1])], axis=1)
     vmem = pl.BlockSpec(memory_space=pltpu.VMEM)
     hbm = pl.BlockSpec(memory_space=pl.ANY)
     out = pl.pallas_call(
         functools.partial(kernel, n_mode, n_space),
-        out_shape=jax.ShapeDtypeStruct((rows, mb, ny), jnp.float32),
-        in_specs=[hbm, vmem, vmem, vmem, hbm, hbm],
+        out_shape=jax.ShapeDtypeStruct((mb * rows * ny // 128, 128), jnp.float32),
+        in_specs=[hbm] * 5,
         out_specs=vmem,
         scratch_shapes=[
             pltpu.VMEM((rows + 2, mb, ny), jnp.bfloat16),
             pltpu.VMEM((sides, rows + 2, mb, ny), jnp.bfloat16),
-            pltpu.VMEM((terms * mb, 4 * mb), jnp.bfloat16),
+            pltpu.VMEM(kappa_x.shape, jnp.float32),
+            pltpu.VMEM(kappa_y.shape, jnp.float32),
+            pltpu.VMEM(coupling.shape, jnp.bfloat16),
+            pltpu.VMEM(pattern.shape, jnp.int32),
+            pltpu.VMEM(coupling.shape[1:], jnp.bfloat16),
+            pltpu.VMEM(pattern.shape[1:], jnp.int32),
+            pltpu.VMEM((terms * mb, 8 * mb), jnp.bfloat16),
             pltpu.VMEM((terms, 8, ny), jnp.float32),
             pltpu.VMEM((mb, ny), jnp.float32),
             pltpu.VMEM((mb, ny), jnp.float32),
+            pltpu.VMEM((mb, ny), jnp.float32),
+            pltpu.VMEM((mb, ny), jnp.float32),
             pltpu.VMEM((1 + sides, mb, ny), jnp.bfloat16),
-            pltpu.SemaphoreType.DMA,
+            pltpu.SemaphoreType.DMA((5,)),
             pltpu.SemaphoreType.DMA((sides, rows)),
             pltpu.SemaphoreType.DMA((sides, rows)),
-            pltpu.SemaphoreType.DMA((8,)),
-            pltpu.SemaphoreType.DMA((8,)),
+            pltpu.SemaphoreType.DMA((9,)),
+            pltpu.SemaphoreType.DMA((9,)),
         ],
-        compiler_params=pltpu.CompilerParams(collective_id=0, has_side_effects=True),
-    )(jnp.swapaxes(field, 0, 1), kappa_x, kappa_y, own, sent, kappa_x)
-    return jnp.swapaxes(out, 0, 1)
+        compiler_params=pltpu.CompilerParams(collective_id=0, has_side_effects=True, vmem_limit_bytes=24 * 2**20),
+    )(jnp.swapaxes(field, 0, 1), kappa_x, kappa_y, coupling, pattern)
+    tiles = out.reshape(mb, rows // 8, ny // 128, 8, 128)
+    return jnp.swapaxes(tiles, 2, 3).reshape(mb, rows, ny)
 
 
 def solution(mesh):

time: 43.1 us -> 37.5 us (0.87)
  local copies, waits for them, and re-layouts: 6.68 us -> 3.25 us
  other arithmetic: 1.88 us -> 0 us
    transpose x3 -> x0, local copies, waits for them, and re-layouts: 4.33 us -> none  [the longest x1 4.13 us: shards(): return jnp.swapaxes(out, 0, 1)]
    unnamed x3 -> x10, local copies, waits for them, and re-layouts: 1.55 us -> 3.25 us
    select_n x1 -> x0, other arithmetic: 1.12 us -> none  [shards(): jnp.where(pattern > 0, coupling, jnp.zeros(coupling.shape, jnp.bfloat16))]
    concatenate x2 -> x0, local copies, waits for them, and re-layouts: 0.79 us -> none  [the longest x1 0.71 us: shards(): jnp.concatenate([jnp.zeros((terms * mb, 3 * mb), jnp.bfloat16), flip(coef...]
    concatenate x1 -> x0, other arithmetic: 0.74 us -> none  [shards(): jnp.concatenate([tall(half), flip(half), tall(coef[1]), jnp.zeros((terms...]
where the time goes in v2:
time: 37.5 us; the launch traced here: 37.3 us
  Pallas kernels  34 us (91%)
  local copies, waits for them, and re-layouts  3.25 us (9%)
    pallas_call x1, Pallas kernels, shards(): pl.pallas_call(functools.partial(kernel, n_mode, n_space), out_shape=jax....  34 us
    unnamed x10, local copies, waits for them, and re-layouts  3.25 us

profile of v2, /device:TPU:0, one launch (start us, length us, event | category | flops | bytes accessed | tf_op | source)
XLA Modules:
  0.0 37.3 jit_solution(6292005448457590038)
XLA Ops:
  0.0 0.0 copy-start.2
  0.0 0.0 copy-start.3
  0.0 0.0 copy-start.1
  0.0 0.0 copy-start
  0.0 1.9 %copy.8 = bf16[32,16,1024]{2,0,1:T(8,128)(2,1)S(1)} copy(bf16[32,16,1024]{2,1,0:T(8,128)(2,1)} %param.5) | data formatting | bytes 2097152 | tf_op args[0]
  1.9 0.0 copy-done.2
  1.9 0.0 copy-done.3
  1.9 0.0 copy-done.1
  2.0 0.0 copy-done
  2.0 34.0 %shard_map.55 = f32[4096,128]{1,0:T(8,128)S(1)} custom-call(bf16[16,32,1024]{2,1,0:T(8,128)(2,1)S(1)} %bitcast.9, f32[8,16,1024]{2,1,0:T(8,128)S(1)} %copy-done, f32[8,16,1024]{2,1,0:T(8,128)S(1)} %copy-done.1, bf16[2,8,32,32]{3,2,1,0:T(8,128)(2,1)S(1)} %copy-done.3, s32[2,8,32,32]{3,2,1,0:T(8,128)S(1)} %copy-done.2), custom_call_target="tpu_custom_call" | custom-call | tf_op jit(solution)/shard_map/pallas_call | solution.py:213
  36.0 1.3 %copy.10 = f32[32,16,1024]{2,1,0:T(8,128)} copy(f32[32,16,1024]{2,1,0:T(8,128)S(1)} %bitcast.8) | data formatting | bytes 4194304
Async XLA Ops:
  0.0 1.9 %copy-start.2 = (s32[2,8,32,32]{3,2,1,0:T(8,128)S(1)}, s32[2,8,32,32]{3,2,1,0:T(8,128)}, u32[]{:S(2)}) copy-start(s32[2,8,32,32]{3,2,1,0:T(8,128)} %pat_hbm.1) | copy-start | bytes 196612
  0.0 1.9 %copy-start.3 = (bf16[2,8,32,32]{3,2,1,0:T(8,128)(2,1)S(1)}, bf16[2,8,32,32]{3,2,1,0:T(8,128)(2,1)}, u32[]{:S(2)}) copy-start(bf16[2,8,32,32]{3,2,1,0:T(8,128)(2,1)} %coup_hbm.1) | copy-start | bytes 98308
  0.0 1.9 %copy-start.1 = (f32[8,16,1024]{2,1,0:T(8,128)S(1)}, f32[8,16,1024]{2,1,0:T(8,128)}, u32[]{:S(2)}) copy-start(f32[8,16,1024]{2,1,0:T(8,128)} %ky_hbm.1) | copy-start | bytes 1572868
  0.0 1.9 %copy-start = (f32[8,16,1024]{2,1,0:T(8,128)S(1)}, f32[8,16,1024]{2,1,0:T(8,128)}, u32[]{:S(2)}) copy-start(f32[8,16,1024]{2,1,0:T(8,128)} %kx_hbm.1) | copy-start | bytes 1572868

commit v3 on v2

--- a/solution.py
+++ b/solution.py
@@ -10,11 +10,12 @@
 LANES = 256
 
 
-def kernel(n_mode, n_space, u_hbm, kx_hbm, ky_hbm, coup_hbm, pat_hbm, out_ref,
-           u_ext, v_ext, kx_ref, ky_ref, coup, pat, coup_in, pat_in, pair_ref,
+def kernel(n_mode, n_space, field_hbm, kx_hbm, ky_hbm, coup_hbm, pat_hbm, out_ref,
+           raw, tall, u_ext, v_ext, kx_ref, ky_ref, coup, pat, packed, packed_in, pair_ref,
            kx_in, fx_prev, fy_row, held, last_row, sh,
            local_sem, main_send, main_recv, halo_send, halo_recv):
-    rows, mb, ny = u_hbm.shape
+    mb, rows, ny = field_hbm.shape
+    group = 128 // mb
     terms = kx_hbm.shape[0]
     sides = v_ext.shape[0]
     mode = lax.axis_index("mode")
@@ -27,6 +28,37 @@
     barrier = pltpu.get_barrier_semaphore()
     for target in (above, below, upper, lower):
         pl.semaphore_signal(barrier, inc=1, device_id=target, device_id_type=pl.DeviceIdType.MESH)
+    locals_ = [
+        pltpu.make_async_copy(src, dst, local_sem.at[i])
+        for i, (src, dst) in enumerate([
+            (field_hbm, raw), (coup_hbm, coup), (pat_hbm, pat), (kx_hbm, kx_ref), (ky_hbm, ky_ref)])]
+    for copy in locals_:
+        copy.start()
+
+    def masked(slot, k):
+        return jnp.where(pat[slot, k] > 0, coup[slot, k].astype(jnp.float32), 0.0)
+
+    def placed(block, shape, offset, flip=False):
+        spot = lax.broadcasted_iota(jnp.int32, shape, 0) + offset
+        place = jnp.where(lax.broadcasted_iota(jnp.int32, shape, 1) == spot, 1.0, 0.0).astype(jnp.bfloat16)
+        return lax.dot_general(block.astype(jnp.bfloat16), place, (((0 if flip else 1,), (0,)), ((), ())),
+                               preferred_element_type=jnp.float32)
+
+    locals_[0].wait()
+    for c in range(0, ny, 128):
+        tall[...] = raw[:, :, c:c + 128].astype(jnp.float32).reshape(mb * rows, 128)
+        for r in range(rows):
+            u_ext[r + 1, :, c:c + 128] = tall[pl.ds(r, mb, stride=rows), :].astype(jnp.bfloat16)
+
+    locals_[1].wait()
+    locals_[2].wait()
+    for q in range(terms // group):
+        beside = None
+        for p in range(group):
+            part = placed(masked(1, q * group + p), (mb, 128), p * mb, flip=True)
+            beside = part if beside is None else beside + part
+        packed[q * mb:(q + 1) * mb] = beside.astype(jnp.bfloat16)
+
     pl.semaphore_wait(barrier, 4)
 
     def remote(src, dst, send, recv, target):
@@ -37,7 +69,7 @@
     towards = (lower, upper)
 
     def row_copy(side, r):
-        return remote(u_hbm.at[r], v_ext.at[side, r + 1], main_send.at[side, r], main_recv.at[side, r], towards[side])
+        return remote(u_ext.at[r + 1], v_ext.at[side, r + 1], main_send.at[side, r], main_recv.at[side, r], towards[side])
 
     def halo_up(side):
         return remote(v_ext.at[side, rows], v_ext.at[side, 0], halo_send.at[4 + side], halo_recv.at[4 + side], above)
@@ -45,17 +77,15 @@
     def halo_down(side):
         return remote(v_ext.at[side, 1], v_ext.at[side, rows + 1], halo_send.at[6 + side], halo_recv.at[6 + side], below)
 
-    coup_copy = remote(coup_hbm.at[1], coup_in, halo_send.at[0], halo_recv.at[0], upper)
-    pat_copy = remote(pat_hbm.at[1], pat_in, halo_send.at[8], halo_recv.at[8], upper)
-    last_copy = remote(u_hbm.at[rows - 1], u_ext.at[0], halo_send.at[1], halo_recv.at[1], above)
-    first_copy = remote(u_hbm.at[0], u_ext.at[rows + 1], halo_send.at[2], halo_recv.at[2], below)
+    coup_copy = remote(packed, packed_in, halo_send.at[0], halo_recv.at[0], upper)
+    last_copy = remote(u_ext.at[rows], u_ext.at[0], halo_send.at[1], halo_recv.at[1], above)
+    first_copy = remote(u_ext.at[1], u_ext.at[rows + 1], halo_send.at[2], halo_recv.at[2], below)
     kx_copy = remote(kx_hbm.at[:, pl.ds(rows - 8, 8), :], kx_in, halo_send.at[3], halo_recv.at[3], above)
 
     for side in range(sides):
         row_copy(side, rows - 1).start()
         row_copy(side, 0).start()
     coup_copy.start()
-    pat_copy.start()
     last_copy.start()
     first_copy.start()
     kx_copy.start()
@@ -63,14 +93,6 @@
         @pl.loop(1, rows - 1)
         def _(r):
             row_copy(side, r).start()
-
-    locals_ = [
-        pltpu.make_async_copy(src, dst, local_sem.at[i])
-        for i, (src, dst) in enumerate([
-            (coup_hbm, coup), (pat_hbm, pat), (u_hbm, u_ext.at[pl.ds(1, rows)]),
-            (kx_hbm, kx_ref), (ky_hbm, ky_ref)])]
-    for copy in locals_:
-        copy.start()
 
     for side in range(sides):
         row_copy(side, rows - 1).wait_recv()
@@ -78,29 +100,17 @@
         row_copy(side, 0).wait_recv()
         halo_down(side).start()
     coup_copy.wait_recv()
-    pat_copy.wait_recv()
-    for copy in locals_:
+    for copy in locals_[3:]:
         copy.wait()
 
-    def masked(values, mask):
-        return jnp.where(mask > 0, values.astype(jnp.float32), 0.0)
-
-    def placed(block, slot, flip):
+    for k in range(terms):
+        q, p = divmod(k, group)
+        half = masked(0, k) * 0.5
         shape = (mb, 4 * mb)
-        spot = lax.broadcasted_iota(jnp.int32, shape, 0) + slot * mb
-        place = jnp.where(lax.broadcasted_iota(jnp.int32, shape, 1) == spot, 1.0, 0.0).astype(jnp.bfloat16)
-        return lax.dot_general(block.astype(jnp.bfloat16), place, (((0 if flip else 1,), (0,)), ((), ())),
-                               preferred_element_type=jnp.float32)
-
-    @pl.loop(0, terms)
-    def _(k):
-        half = masked(coup[0, k], pat[0, k]) * 0.5
-        coef = (placed(half, 0, False) + placed(half, 1, True)
-                + placed(masked(coup[1, k], pat[1, k]), 2, False)
-                + placed(masked(coup_in[k], pat_in[k]), 3, True)).astype(jnp.bfloat16)
-        at = pl.ds(pl.multiple_of(k * mb, mb), mb)
-        pair_ref[at, :4 * mb] = coef
-        pair_ref[at, 4 * mb:] = -coef
+        coef = (placed(half, shape, 0) + placed(half, shape, mb, flip=True) + placed(masked(1, k), shape, 2 * mb)
+                + placed(packed_in[q * mb:(q + 1) * mb, p * mb:(p + 1) * mb], shape, 3 * mb)).astype(jnp.bfloat16)
+        pair_ref[k * mb:(k + 1) * mb, :4 * mb] = coef
+        pair_ref[k * mb:(k + 1) * mb, 4 * mb:] = -coef
 
     last_copy.wait_recv()
     first_copy.wait_recv()
@@ -200,7 +210,7 @@
             row_copy(side, r).wait_send()
         halo_up(side).wait_send()
         halo_down(side).wait_send()
-    for copy in (coup_copy, pat_copy, last_copy, first_copy, kx_copy):
+    for copy in (coup_copy, last_copy, first_copy, kx_copy):
         copy.wait_send()
 
 
@@ -209,21 +219,23 @@
     terms = kappa_x.shape[0]
     sides = 1 if n_mode == 2 else 2
     vmem = pl.BlockSpec(memory_space=pltpu.VMEM)
-    hbm = pl.BlockSpec(memory_space=pl.ANY)
+    hbm = pl.BlockSpec(memory_space=pltpu.HBM)
     out = pl.pallas_call(
         functools.partial(kernel, n_mode, n_space),
         out_shape=jax.ShapeDtypeStruct((mb * rows * ny // 128, 128), jnp.float32),
         in_specs=[hbm] * 5,
         out_specs=vmem,
         scratch_shapes=[
+            pltpu.VMEM(field.shape, jnp.bfloat16),
+            pltpu.VMEM((mb * rows, 128), jnp.float32),
             pltpu.VMEM((rows + 2, mb, ny), jnp.bfloat16),
             pltpu.VMEM((sides, rows + 2, mb, ny), jnp.bfloat16),
             pltpu.VMEM(kappa_x.shape, jnp.float32),
             pltpu.VMEM(kappa_y.shape, jnp.float32),
             pltpu.VMEM(coupling.shape, jnp.bfloat16),
             pltpu.VMEM(pattern.shape, jnp.int32),
-            pltpu.VMEM(coupling.shape[1:], jnp.bfloat16),
-            pltpu.VMEM(pattern.shape[1:], jnp.int32),
+            pltpu.VMEM((terms * mb * mb // 128, 128), jnp.bfloat16),
+            pltpu.VMEM((terms * mb * mb // 128, 128), jnp.bfloat16),
             pltpu.VMEM((terms * mb, 8 * mb), jnp.bfloat16),
             pltpu.VMEM((terms, 8, ny), jnp.float32),
             pltpu.VMEM((mb, ny), jnp.float32),
@@ -238,7 +250,8 @@
             pltpu.SemaphoreType.DMA((9,)),
         ],
         compiler_params=pltpu.CompilerParams(collective_id=0, has_side_effects=True, vmem_limit_bytes=24 * 2**20),
-    )(jnp.swapaxes(field, 0, 1), kappa_x, kappa_y, coupling, pattern)
+    )(*[pltpu.with_memory_space_constraint(x, pltpu.HBM)
+        for x in (field, kappa_x, kappa_y, coupling, pattern)])
     tiles = out.reshape(mb, rows // 8, ny // 128, 8, 128)
     return jnp.swapaxes(tiles, 2, 3).reshape(mb, rows, ny)
 

time: 37.5 us -> 32 us (0.85)
  Pallas kernels: 34 us -> 30.6 us
  local copies, waits for them, and re-layouts: 3.25 us -> 1.32 us
    pallas_call x1, Pallas kernels: 34 us -> 30.6 us  [shards(): pl.pallas_call(functools.partial(kernel, n_mode, n_space), out_shape=jax....]
    unnamed x10 -> x1, local copies, waits for them, and re-layouts: 3.25 us -> 1.32 us
where the time goes in v3:
time: 32 us; the launch traced here: 31.9 us
  Pallas kernels  30.6 us (96%)
  local copies, waits for them, and re-layouts  1.32 us (4%)
    pallas_call x1, Pallas kernels, shards(): pl.pallas_call(functools.partial(kernel, n_mode, n_space), out_shape=jax....  30.6 us
    unnamed x1, local copies, waits for them, and re-layouts  1.32 us

profile of v3, /device:TPU:0, one launch (start us, length us, event | category | flops | bytes accessed | tf_op | source)
XLA Modules:
  0.0 31.9 jit_solution(3555154000837524904)
XLA Ops:
  0.0 30.6 %shard_map.55 = f32[4096,128]{1,0:T(8,128)S(1)} custom-call(bf16[32,16,1024]{2,1,0:T(8,128)(2,1)} %field_hbm.1, f32[8,16,1024]{2,1,0:T(8,128)} %kx_hbm.1, f32[8,16,1024]{2,1,0:T(8,128)} %ky_hbm.1, bf16[2,8,32,32]{3,2,1,0:T(8,128)(2,1)} %coup_hbm.1, s32[2,8,32,32]{3,2,1,0:T(8,128)} %pat_hbm.1), custom_call_target="tpu_custom_call" | custom-call | tf_op jit(solution)/shard_map/pallas_call | solution.py:223
  30.6 1.3 %copy.7 = f32[32,16,1024]{2,1,0:T(8,128)} copy(f32[32,16,1024]{2,1,0:T(8,128)S(1)} %bitcast.5) | data formatting | bytes 4194304

commit v4 on v3

--- a/solution.py
+++ b/solution.py
@@ -8,12 +8,13 @@
 from jax.sharding import PartitionSpec as P
 
 LANES = 256
+HEAD = 128
 
 
 def kernel(n_mode, n_space, field_hbm, kx_hbm, ky_hbm, coup_hbm, pat_hbm, out_ref,
-           raw, tall, u_ext, v_ext, kx_ref, ky_ref, coup, pat, packed, packed_in, pair_ref,
+           raw, tall, v_raw, u_ext, v_ext, kx_ref, ky_ref, coup, pat, packed, packed_in, pair_ref,
            kx_in, fx_prev, fy_row, held, last_row, sh,
-           local_sem, main_send, main_recv, halo_send, halo_recv):
+           local_sem, head_send, head_recv, main_send, main_recv, halo_send, halo_recv):
     mb, rows, ny = field_hbm.shape
     group = 128 // mb
     terms = kx_hbm.shape[0]
@@ -35,6 +36,33 @@
     for copy in locals_:
         copy.start()
 
+    pl.semaphore_wait(barrier, 4)
+
+    def remote(src, dst, send, recv, target):
+        return pltpu.make_async_remote_copy(
+            src_ref=src, dst_ref=dst, send_sem=send, recv_sem=recv,
+            device_id=target, device_id_type=pl.DeviceIdType.MESH)
+
+    towards = (lower, upper)
+
+    def row_copy(side, r):
+        rest = pl.ds(HEAD, ny - HEAD)
+        return remote(u_ext.at[r + 1, :, rest], v_ext.at[side, r + 1, :, rest], main_send.at[side, r], main_recv.at[side, r], towards[side])
+
+    def head_copy(side):
+        return remote(field_hbm.at[:, :, pl.ds(0, HEAD)], v_raw.at[side], head_send.at[side], head_recv.at[side], towards[side])
+
+    def halo_up(side):
+        return remote(v_ext.at[side, rows], v_ext.at[side, 0], halo_send.at[4 + side], halo_recv.at[4 + side], above)
+
+    def halo_down(side):
+        return remote(v_ext.at[side, 1], v_ext.at[side, rows + 1], halo_send.at[6 + side], halo_recv.at[6 + side], below)
+
+    kx_copy = remote(kx_hbm.at[:, pl.ds(rows - 8, 8), :], kx_in, halo_send.at[3], halo_recv.at[3], above)
+    for side in range(sides):
+        head_copy(side).start()
+    kx_copy.start()
+
     def masked(slot, k):
         return jnp.where(pat[slot, k] > 0, coup[slot, k].astype(jnp.float32), 0.0)
 
@@ -43,12 +71,6 @@
         place = jnp.where(lax.broadcasted_iota(jnp.int32, shape, 1) == spot, 1.0, 0.0).astype(jnp.bfloat16)
         return lax.dot_general(block.astype(jnp.bfloat16), place, (((0 if flip else 1,), (0,)), ((), ())),
                                preferred_element_type=jnp.float32)
-
-    locals_[0].wait()
-    for c in range(0, ny, 128):
-        tall[...] = raw[:, :, c:c + 128].astype(jnp.float32).reshape(mb * rows, 128)
-        for r in range(rows):
-            u_ext[r + 1, :, c:c + 128] = tall[pl.ds(r, mb, stride=rows), :].astype(jnp.bfloat16)
 
     locals_[1].wait()
     locals_[2].wait()
@@ -59,28 +81,18 @@
             beside = part if beside is None else beside + part
         packed[q * mb:(q + 1) * mb] = beside.astype(jnp.bfloat16)
 
-    pl.semaphore_wait(barrier, 4)
-
-    def remote(src, dst, send, recv, target):
-        return pltpu.make_async_remote_copy(
-            src_ref=src, dst_ref=dst, send_sem=send, recv_sem=recv,
-            device_id=target, device_id_type=pl.DeviceIdType.MESH)
-
-    towards = (lower, upper)
-
-    def row_copy(side, r):
-        return remote(u_ext.at[r + 1], v_ext.at[side, r + 1], main_send.at[side, r], main_recv.at[side, r], towards[side])
-
-    def halo_up(side):
-        return remote(v_ext.at[side, rows], v_ext.at[side, 0], halo_send.at[4 + side], halo_recv.at[4 + side], above)
-
-    def halo_down(side):
-        return remote(v_ext.at[side, 1], v_ext.at[side, rows + 1], halo_send.at[6 + side], halo_recv.at[6 + side], below)
+    def by_rows(source, source_at, target, at):
+        tall[...] = source[:, :, source_at:source_at + 128].astype(jnp.float32).reshape(mb * rows, 128)
+        for r in range(rows):
+            target[r + 1, :, at:at + 128] = tall[pl.ds(r, mb, stride=rows), :].astype(jnp.bfloat16)
+
+    locals_[0].wait()
+    for c in range(0, ny, 128):
+        by_rows(raw, c, u_ext, c)
 
     coup_copy = remote(packed, packed_in, halo_send.at[0], halo_recv.at[0], upper)
     last_copy = remote(u_ext.at[rows], u_ext.at[0], halo_send.at[1], halo_recv.at[1], above)
     first_copy = remote(u_ext.at[1], u_ext.at[rows + 1], halo_send.at[2], halo_recv.at[2], below)
-    kx_copy = remote(kx_hbm.at[:, pl.ds(rows - 8, 8), :], kx_in, halo_send.at[3], halo_recv.at[3], above)
 
     for side in range(sides):
         row_copy(side, rows - 1).start()
@@ -88,12 +100,15 @@
     coup_copy.start()
     last_copy.start()
     first_copy.start()
-    kx_copy.start()
     for side in range(sides):
         @pl.loop(1, rows - 1)
         def _(r):
             row_copy(side, r).start()
 
+    for side in range(sides):
+        head_copy(side).wait_recv()
+        for c in range(0, HEAD, 128):
+            by_rows(v_raw.at[side], c, v_ext.at[side], c)
     for side in range(sides):
         row_copy(side, rows - 1).wait_recv()
         halo_up(side).start()
@@ -208,6 +223,7 @@
         @pl.loop(0, rows)
         def _(r):
             row_copy(side, r).wait_send()
+        head_copy(side).wait_send()
         halo_up(side).wait_send()
         halo_down(side).wait_send()
     for copy in (coup_copy, last_copy, first_copy, kx_copy):
@@ -228,6 +244,7 @@
         scratch_shapes=[
             pltpu.VMEM(field.shape, jnp.bfloat16),
             pltpu.VMEM((mb * rows, 128), jnp.float32),
+            pltpu.VMEM((sides, mb, rows, HEAD), jnp.bfloat16),
             pltpu.VMEM((rows + 2, mb, ny), jnp.bfloat16),
             pltpu.VMEM((sides, rows + 2, mb, ny), jnp.bfloat16),
             pltpu.VMEM(kappa_x.shape, jnp.float32),
@@ -244,6 +261,8 @@
             pltpu.VMEM((mb, ny), jnp.float32),
             pltpu.VMEM((1 + sides, mb, ny), jnp.bfloat16),
             pltpu.SemaphoreType.DMA((5,)),
+            pltpu.SemaphoreType.DMA((sides,)),
+            pltpu.SemaphoreType.DMA((sides,)),
             pltpu.SemaphoreType.DMA((sides, rows)),
             pltpu.SemaphoreType.DMA((sides, rows)),
             pltpu.SemaphoreType.DMA((9,)),

time: 32 us -> 32.3 us (level)
  no operation moved by 1% of the time
where the time goes in v4:
time: 32.3 us; the launch traced here: 32.2 us
  Pallas kernels  30.9 us (96%)
  local copies, waits for them, and re-layouts  1.32 us (4%)
    pallas_call x1, Pallas kernels, shards(): pl.pallas_call(functools.partial(kernel, n_mode, n_space), out_shape=jax....  30.9 us
    unnamed x1, local copies, waits for them, and re-layouts  1.32 us

profile of v4, /device:TPU:0, one launch (start us, length us, event | category | flops | bytes accessed | tf_op | source)
XLA Modules:
  0.0 32.2 jit_solution(3550019870099097268)
XLA Ops:
  0.0 30.9 %shard_map.55 = f32[4096,128]{1,0:T(8,128)S(1)} custom-call(bf16[32,16,1024]{2,1,0:T(8,128)(2,1)} %field_hbm.1, f32[8,16,1024]{2,1,0:T(8,128)} %kx_hbm.1, f32[8,16,1024]{2,1,0:T(8,128)} %ky_hbm.1, bf16[2,8,32,32]{3,2,1,0:T(8,128)(2,1)} %coup_hbm.1, s32[2,8,32,32]{3,2,1,0:T(8,128)} %pat_hbm.1), custom_call_target="tpu_custom_call" | custom-call | tf_op jit(solution)/shard_map/pallas_call | solution.py:239
  30.9 1.3 %copy.7 = f32[32,16,1024]{2,1,0:T(8,128)} copy(f32[32,16,1024]{2,1,0:T(8,128)S(1)} %bitcast.5) | data formatting | bytes 4194304

commit v5 on v4

--- a/solution.py
+++ b/solution.py
@@ -14,7 +14,7 @@
 def kernel(n_mode, n_space, field_hbm, kx_hbm, ky_hbm, coup_hbm, pat_hbm, out_ref,
            raw, tall, v_raw, u_ext, v_ext, kx_ref, ky_ref, coup, pat, packed, packed_in, pair_ref,
            kx_in, fx_prev, fy_row, held, last_row, sh,
-           local_sem, head_send, head_recv, main_send, main_recv, halo_send, halo_recv):
+           local_sem, head_send, head_recv, piece_send, piece_recv, main_send, main_recv, halo_send, halo_recv):
     mb, rows, ny = field_hbm.shape
     group = 128 // mb
     terms = kx_hbm.shape[0]
@@ -49,6 +49,12 @@
         rest = pl.ds(HEAD, ny - HEAD)
         return remote(u_ext.at[r + 1, :, rest], v_ext.at[side, r + 1, :, rest], main_send.at[side, r], main_recv.at[side, r], towards[side])
 
+    order = list(reversed(range(ny // LANES)))
+
+    def piece_copy(side, b):
+        cols = pl.ds(max(b * LANES, HEAD), min(LANES, (b + 1) * LANES - HEAD))
+        return remote(u_ext.at[rows - 1, :, cols], v_ext.at[side, rows - 1, :, cols], piece_send.at[side, b], piece_recv.at[side, b], towards[side])
+
     def head_copy(side):
         return remote(field_hbm.at[:, :, pl.ds(0, HEAD)], v_raw.at[side], head_send.at[side], head_recv.at[side], towards[side])
 
@@ -101,9 +107,11 @@
     last_copy.start()
     first_copy.start()
     for side in range(sides):
-        @pl.loop(1, rows - 1)
+        @pl.loop(1, rows - 2)
         def _(r):
             row_copy(side, r).start()
+        for b in order:
+            piece_copy(side, b).start()
 
     for side in range(sides):
         head_copy(side).wait_recv()
@@ -172,16 +180,19 @@
     def kx_row(r, cols):
         return lambda k: kx_ref[k, pl.ds(r, 1), cols]
 
+    def block_flux_y(r, cols):
+        ahead = [sh[0, :, cols]] * 2 + [sh[1, :, cols], sh[sides, :, cols]]
+        diff = jnp.dot(pair, jnp.concatenate(ahead + stack(r + 1, cols), axis=0),
+                       preferred_element_type=jnp.float32)
+        return weighted(diff, lambda k: ky_ref[k, pl.ds(r, 1), cols])
+
     def flux_y_part(r):
         e = r + 1
         sh[0] = shifted(u_ext[e])
         for side in range(sides):
             sh[1 + side] = shifted(v_ext[side, e])
         for cols in blocks:
-            ahead = [sh[0, :, cols]] * 2 + [sh[1, :, cols], sh[sides, :, cols]]
-            diff = jnp.dot(pair, jnp.concatenate(ahead + stack(e, cols), axis=0),
-                           preferred_element_type=jnp.float32)
-            fy_row[:, cols] = weighted(diff, lambda k: ky_ref[k, pl.ds(r, 1), cols])
+            fy_row[:, cols] = block_flux_y(r, cols)
         fy = fy_row[...]
         lane = lax.broadcasted_iota(jnp.int32, fy.shape, 1)
         return jnp.where(lane == 0, 0.0, pltpu.roll(fy, 1, axis=1)) - fy
@@ -211,18 +222,45 @@
         flux_x_step(r)
 
     held[...] = flux_y_part(rows - 3)
-    for side in range(sides):
-        row_copy(side, rows - 2).wait_recv()
-    flux_x_step(rows - 3)
-    held[...] = flux_y_part(rows - 2)
-    flux_x_step(rows - 2)
-    for cols in blocks:
-        put(final, cols, last_row[:, cols] + fx_prev[:, cols])
-
-    for side in range(sides):
-        @pl.loop(0, rows)
+    e = rows - 1
+    sh[0] = shifted(u_ext[e])
+
+    def finish(b):
+        start = b * LANES - (0 if b == 0 else 128)
+        fy = fy_row[:, start:(b + 1) * LANES]
+        moved = pltpu.roll(fy, 1, axis=1)
+        if b == 0:
+            moved = jnp.where(lax.broadcasted_iota(jnp.int32, fy.shape, 1) == 0, 0.0, moved)
+        value = (moved - fy)[:, fy.shape[1] - LANES:]
+        put(rows - 2, blocks[b], held[:, blocks[b]] + value)
+
+    for b in order:
+        cols = blocks[b]
+        last = b == order[0]
+        for side in range(sides):
+            piece_copy(side, b).wait_recv()
+            window = v_ext[side, e, :, b * LANES:(b + 1) * LANES + (0 if last else 128)].astype(jnp.float32)
+            moved = pltpu.roll(window, window.shape[1] - 1, axis=1)
+            if last:
+                moved = jnp.where(lax.broadcasted_iota(jnp.int32, window.shape, 1) == LANES - 1, 0.0, moved)
+            sh[1 + side, :, cols] = moved[:, :LANES].astype(jnp.bfloat16)
+        before = flux_x(rows - 2, cols, kx_row(rows - 3, cols))
+        fx = flux_x(e, cols, kx_row(rows - 2, cols))
+        fy_row[:, cols] = block_flux_y(rows - 2, cols)
+        put(rows - 3, cols, fx_prev[:, cols] - before + held[:, cols])
+        held[:, cols] = before - fx
+        put(final, cols, last_row[:, cols] + fx)
+        if not last:
+            finish(b + 1)
+    finish(0)
+
+    for side in range(sides):
+        @pl.loop(0, rows - 2)
         def _(r):
             row_copy(side, r).wait_send()
+        row_copy(side, rows - 1).wait_send()
+        for b in order:
+            piece_copy(side, b).wait_send()
         head_copy(side).wait_send()
         halo_up(side).wait_send()
         halo_down(side).wait_send()
@@ -263,6 +301,8 @@
             pltpu.SemaphoreType.DMA((5,)),
             pltpu.SemaphoreType.DMA((sides,)),
             pltpu.SemaphoreType.DMA((sides,)),
+            pltpu.SemaphoreType.DMA((sides, ny // LANES)),
+            pltpu.SemaphoreType.DMA((sides, ny // LANES)),
             pltpu.SemaphoreType.DMA((sides, rows)),
             pltpu.SemaphoreType.DMA((sides, rows)),
             pltpu.SemaphoreType.DMA((9,)),

time: 32.3 us -> 33.1 us (1.025)
  Pallas kernels: 30.9 us -> 31.6 us
    pallas_call x1, Pallas kernels: 30.9 us -> 31.6 us  [shards(): pl.pallas_call(functools.partial(kernel, n_mode, n_space), out_shape=jax....]
where the time goes in v5:
time: 33.1 us; the launch traced here: 33 us
  Pallas kernels  31.6 us (95%)
  local copies, waits for them, and re-layouts  1.32 us (4%)
    pallas_call x1, Pallas kernels, shards(): pl.pallas_call(functools.partial(kernel, n_mode, n_space), out_shape=jax....  31.6 us
    unnamed x1, local copies, waits for them, and re-layouts  1.32 us

profile of v5, /device:TPU:0, one launch (start us, length us, event | category | flops | bytes accessed | tf_op | source)
XLA Modules:
  0.0 33.0 jit_solution(13074448222639386847)
XLA Ops:
  0.0 31.6 %shard_map.55 = f32[4096,128]{1,0:T(8,128)S(1)} custom-call(bf16[32,16,1024]{2,1,0:T(8,128)(2,1)} %field_hbm.1, f32[8,16,1024]{2,1,0:T(8,128)} %kx_hbm.1, f32[8,16,1024]{2,1,0:T(8,128)} %ky_hbm.1, bf16[2,8,32,32]{3,2,1,0:T(8,128)(2,1)} %coup_hbm.1, s32[2,8,32,32]{3,2,1,0:T(8,128)} %pat_hbm.1), custom_call_target="tpu_custom_call" | custom-call | tf_op jit(solution)/shard_map/pallas_call | solution.py:277
  31.6 1.3 %copy.7 = f32[32,16,1024]{2,1,0:T(8,128)} copy(f32[32,16,1024]{2,1,0:T(8,128)S(1)} %bitcast.5) | data formatting | bytes 4194304

commit v6 on v3

--- a/solution.py
+++ b/solution.py
@@ -31,7 +31,9 @@
     locals_ = [
         pltpu.make_async_copy(src, dst, local_sem.at[i])
         for i, (src, dst) in enumerate([
-            (field_hbm, raw), (coup_hbm, coup), (pat_hbm, pat), (kx_hbm, kx_ref), (ky_hbm, ky_ref)])]
+            (field_hbm.at[:, pl.ds(0, 8), :], raw.at[:, pl.ds(0, 8), :]),
+            (field_hbm.at[:, pl.ds(8, rows - 8), :], raw.at[:, pl.ds(8, rows - 8), :]),
+            (coup_hbm, coup), (pat_hbm, pat), (kx_hbm, kx_ref), (ky_hbm, ky_ref)])]
     for copy in locals_:
         copy.start()
 
@@ -44,14 +46,51 @@
         return lax.dot_general(block.astype(jnp.bfloat16), place, (((0 if flip else 1,), (0,)), ((), ())),
                                preferred_element_type=jnp.float32)
 
+    def by_rows(first, count):
+        for c in range(0, ny, 128):
+            tall[:mb * count] = raw[:, first:first + count, c:c + 128].astype(jnp.float32).reshape(mb * count, 128)
+            for r in range(count):
+                u_ext[first + r + 1, :, c:c + 128] = tall[pl.ds(r, mb, stride=count), :].astype(jnp.bfloat16)
+
     locals_[0].wait()
-    for c in range(0, ny, 128):
-        tall[...] = raw[:, :, c:c + 128].astype(jnp.float32).reshape(mb * rows, 128)
-        for r in range(rows):
-            u_ext[r + 1, :, c:c + 128] = tall[pl.ds(r, mb, stride=rows), :].astype(jnp.bfloat16)
-
+    by_rows(0, 8)
+    pl.semaphore_wait(barrier, 4)
+
+    def remote(src, dst, send, recv, target):
+        return pltpu.make_async_remote_copy(
+            src_ref=src, dst_ref=dst, send_sem=send, recv_sem=recv,
+            device_id=target, device_id_type=pl.DeviceIdType.MESH)
+
+    towards = (lower, upper)
+
+    def row_copy(side, r):
+        return remote(u_ext.at[r + 1], v_ext.at[side, r + 1], main_send.at[side, r], main_recv.at[side, r], towards[side])
+
+    def halo_up(side):
+        return remote(v_ext.at[side, rows], v_ext.at[side, 0], halo_send.at[4 + side], halo_recv.at[4 + side], above)
+
+    def halo_down(side):
+        return remote(v_ext.at[side, 1], v_ext.at[side, rows + 1], halo_send.at[6 + side], halo_recv.at[6 + side], below)
+
+    coup_copy = remote(packed, packed_in, halo_send.at[0], halo_recv.at[0], upper)
+    last_copy = remote(u_ext.at[rows], u_ext.at[0], halo_send.at[1], halo_recv.at[1], above)
+    first_copy = remote(u_ext.at[1], u_ext.at[rows + 1], halo_send.at[2], halo_recv.at[2], below)
+    kx_copy = remote(kx_hbm.at[:, pl.ds(rows - 8, 8), :], kx_in, halo_send.at[3], halo_recv.at[3], above)
+
+    for side in range(sides):
+        row_copy(side, 0).start()
+    first_copy.start()
+    kx_copy.start()
     locals_[1].wait()
+    by_rows(8, rows - 8)
+    for side in range(sides):
+        row_copy(side, rows - 1).start()
+        row_copy(side, 1).start()
+        row_copy(side, 2).start()
+    last_copy.start()
+
     locals_[2].wait()
+    locals_[3].wait()
     for q in range(terms // group):
         beside = None
         for p in range(group):
@@ -59,48 +98,19 @@
             beside = part if beside is None else beside + part
         packed[q * mb:(q + 1) * mb] = beside.astype(jnp.bfloat16)
 
-    pl.semaphore_wait(barrier, 4)
-
-    def remote(src, dst, send, recv, target):
-        return pltpu.make_async_remote_copy(
-            src_ref=src, dst_ref=dst, send_sem=send, recv_sem=recv,
-            device_id=target, device_id_type=pl.DeviceIdType.MESH)
-
-    towards = (lower, upper)
-
-    def row_copy(side, r):
-        return remote(u_ext.at[r + 1], v_ext.at[side, r + 1], main_send.at[side, r], main_recv.at[side, r], towards[side])
-
-    def halo_up(side):
-        return remote(v_ext.at[side, rows], v_ext.at[side, 0], halo_send.at[4 + side], halo_recv.at[4 + side], above)
-
-    def halo_down(side):
-        return remote(v_ext.at[side, 1], v_ext.at[side, rows + 1], halo_send.at[6 + side], halo_recv.at[6 + side], below)
-
-    coup_copy = remote(packed, packed_in, halo_send.at[0], halo_recv.at[0], upper)
-    last_copy = remote(u_ext.at[rows], u_ext.at[0], halo_send.at[1], halo_recv.at[1], above)
-    first_copy = remote(u_ext.at[1], u_ext.at[rows + 1], halo_send.at[2], halo_recv.at[2], below)
-    kx_copy = remote(kx_hbm.at[:, pl.ds(rows - 8, 8), :], kx_in, halo_send.at[3], halo_recv.at[3], above)
-
-    for side in range(sides):
-        row_copy(side, rows - 1).start()
-        row_copy(side, 0).start()
     coup_copy.start()
-    last_copy.start()
-    first_copy.start()
-    kx_copy.start()
-    for side in range(sides):
-        @pl.loop(1, rows - 1)
+    for side in range(sides):
+        @pl.loop(3, rows - 1)
         def _(r):
             row_copy(side, r).start()
 
     for side in range(sides):
+        row_copy(side, 0).wait_recv()
+        halo_down(side).start()
         row_copy(side, rows - 1).wait_recv()
         halo_up(side).start()
-        row_copy(side, 0).wait_recv()
-        halo_down(side).start()
     coup_copy.wait_recv()
-    for copy in locals_[3:]:
+    for copy in locals_[4:]:
         copy.wait()
 
     for k in range(terms):
@@ -243,7 +253,7 @@
             pltpu.VMEM((mb, ny), jnp.float32),
             pltpu.VMEM((mb, ny), jnp.float32),
             pltpu.VMEM((1 + sides, mb, ny), jnp.bfloat16),
-            pltpu.SemaphoreType.DMA((5,)),
+            pltpu.SemaphoreType.DMA((6,)),
             pltpu.SemaphoreType.DMA((sides, rows)),
             pltpu.SemaphoreType.DMA((sides, rows)),
             pltpu.SemaphoreType.DMA((9,)),

time: 32 us -> 31.6 us (0.988)
  Pallas kernels: 30.6 us -> 30.1 us
    pallas_call x1, Pallas kernels: 30.6 us -> 30.1 us  [shards(): pl.pallas_call(functools.partial(kernel, n_mode, n_space), out_shape=jax....]
where the time goes in v6:
time: 31.6 us; the launch traced here: 31.5 us
  Pallas kernels  30.1 us (95%)
  local copies, waits for them, and re-layouts  1.32 us (4%)
    pallas_call x1, Pallas kernels, shards(): pl.pallas_call(functools.partial(kernel, n_mode, n_space), out_shape=jax....  30.1 us
    unnamed x1, local copies, waits for them, and re-layouts  1.32 us

profile of v6, /device:TPU:0, one launch (start us, length us, event | category | flops | bytes accessed | tf_op | source)
XLA Modules:
  0.0 31.5 jit_solution(3320713700859183162)
XLA Ops:
  0.0 30.1 %shard_map.55 = f32[4096,128]{1,0:T(8,128)S(1)} custom-call(bf16[32,16,1024]{2,1,0:T(8,128)(2,1)} %field_hbm.1, f32[8,16,1024]{2,1,0:T(8,128)} %kx_hbm.1, f32[8,16,1024]{2,1,0:T(8,128)} %ky_hbm.1, bf16[2,8,32,32]{3,2,1,0:T(8,128)(2,1)} %coup_hbm.1, s32[2,8,32,32]{3,2,1,0:T(8,128)} %pat_hbm.1), custom_call_target="tpu_custom_call" | custom-call | tf_op jit(solution)/shard_map/pallas_call | solution.py:233
  30.1 1.3 %copy.7 = f32[32,16,1024]{2,1,0:T(8,128)} copy(f32[32,16,1024]{2,1,0:T(8,128)S(1)} %bitcast.5) | data formatting | bytes 4194304

commit v7 on v6

--- a/solution.py
+++ b/solution.py
@@ -7,7 +7,7 @@
 from jax.experimental.pallas import tpu as pltpu
 from jax.sharding import PartitionSpec as P
 
-LANES = 256
+LANES = 512
 
 
 def kernel(n_mode, n_space, field_hbm, kx_hbm, ky_hbm, coup_hbm, pat_hbm, out_ref,

time: 31.6 us -> 31.6 us (level)
  no operation moved by 1% of the time
where the time goes in v7:
time: 31.6 us; the launch traced here: 31.5 us
  Pallas kernels  30.1 us (95%)
  local copies, waits for them, and re-layouts  1.32 us (4%)
    pallas_call x1, Pallas kernels, shards(): pl.pallas_call(functools.partial(kernel, n_mode, n_space), out_shape=jax....  30.1 us
    unnamed x1, local copies, waits for them, and re-layouts  1.32 us

profile of v7, /device:TPU:0, one launch (start us, length us, event | category | flops | bytes accessed | tf_op | source)
XLA Modules:
  0.0 31.5 jit_solution(11591549961627816773)
XLA Ops:
  0.0 30.1 %shard_map.55 = f32[4096,128]{1,0:T(8,128)S(1)} custom-call(bf16[32,16,1024]{2,1,0:T(8,128)(2,1)} %field_hbm.1, f32[8,16,1024]{2,1,0:T(8,128)} %kx_hbm.1, f32[8,16,1024]{2,1,0:T(8,128)} %ky_hbm.1, bf16[2,8,32,32]{3,2,1,0:T(8,128)(2,1)} %coup_hbm.1, s32[2,8,32,32]{3,2,1,0:T(8,128)} %pat_hbm.1), custom_call_target="tpu_custom_call" | custom-call | tf_op jit(solution)/shard_map/pallas_call | solution.py:233
  30.1 1.3 %copy.7 = f32[32,16,1024]{2,1,0:T(8,128)} copy(f32[32,16,1024]{2,1,0:T(8,128)S(1)} %bitcast.5) | data formatting | bytes 4194304
